TPU v7x, 32 devices: a whole 2x2x4 slice. The times are simulated.
32 devices in a mesh: scene: 4 (over x, core), seq: 8 (over z, y).
Axes of the slice: x: 2, y: 2, z: 4, core: 2. Of those that a mesh axis runs over, the one named last changes fastest.
Arguments:
- tokens: bfloat16 [10240, 768], P(('scene', 'seq')), may hold values from -6 to 6
- scene_tokens: int32 [4], P('scene'), may hold values from 128 to 320, as said below
- cotangent: bfloat16 [10240, 768], P(('scene', 'seq')), may hold values from -6 to 6
- qkv_master: float32 [768, 2304], P(('scene', 'seq')), may hold values from -0.21875 to 0.21875
- out_master: float32 [768, 768], P(('scene', 'seq')), may hold values from -6 to 6
- up_master: float32 [768, 3072], P(('scene', 'seq')), may hold values from -0.21875 to 0.21875
- down_master: float32 [3072, 768], P(('scene', 'seq')), may hold values from -0.109375 to 0.109375
- gain_one: float32 [768], replicated, may hold values from 0.5 to 1.5
- gain_two: float32 [768], replicated, may hold values from 0.5 to 1.5
Outputs:
- mixed: bfloat16 [10240, 768], P(('scene', 'seq'))
- input_grad: float32 [10240, 768], P(('scene', 'seq'))
- qkv_grad: float32 [768, 2304], P(('scene', 'seq'))
- out_grad: float32 [768, 768], P(('scene', 'seq'))
- up_grad: float32 [768, 3072], P(('scene', 'seq'))
- down_grad: float32 [3072, 768], P(('scene', 'seq'))
- gain_one_grad: float32 [768], P(('scene', 'seq'))
- gain_two_grad: float32 [768], P(('scene', 'seq'))
Inputs may be any that keep to these rules, and one draw needn't show every extreme that they name: Slots 0 to scene_tokens[s] - 1 of every device of scene s's group hold that scene's tokens, the others are padding; one scene, drawn from the seed, has all 320 slots of every device live.
All inputs are finite; a program needn't handle non-finite values.
Results may differ from a plain program's by a relative error of at most 0.02.
Values may be sent and summed in bfloat16 or wider, within the bound.
No kernel may reach another device: no remote copies, remote signals or barrier semaphores. Data moves between devices by JAX's collectives and lax.ppermute only.
A program may use at most 512 MiB of HBM per device.

v0:
```python
import jax
import jax.numpy as jnp
from jax import lax
from jax.sharding import PartitionSpec as P

HEADS = 12
HEAD = 64
NEG_BIG = -1e30


def norm_rows(values, gain_vector):
    mean_value = jnp.mean(values, axis=-1, keepdims=True)
    centered = values - mean_value
    variance = jnp.mean(centered * centered, axis=-1, keepdims=True)
    inverse = lax.rsqrt(variance + 1e-05)
    scaled = centered * inverse
    return (scaled * gain_vector, scaled, inverse)


def norm_back(grad_result, scaled, inverse, gain_vector):
    grad_scaled = grad_result * gain_vector
    first_mean = jnp.mean(grad_scaled, axis=-1, keepdims=True)
    second_mean = jnp.mean(grad_scaled * scaled, axis=-1, keepdims=True)
    grad_input = inverse * (grad_scaled - first_mean - scaled * second_mean)
    return (grad_input, jnp.sum(grad_result * scaled, axis=0))


def split_heads(values):
    return values.reshape(values.shape[0], HEADS, HEAD)


def score_grads(query_part, grad_part, key_part, value_part, lse_part, delta_part, live_keys):
    scores = (
        jnp.einsum("qhd,khd->hqk", query_part, key_part, preferred_element_type=jnp.float32) * 0.125
    )
    weights_now = jnp.where(live_keys[None, None, :], jnp.exp(scores - lse_part[:, :, None]), 0.0)
    grad_weights = jnp.einsum(
        "qhd,khd->hqk", grad_part, value_part, preferred_element_type=jnp.float32
    )
    dscore = (weights_now * (grad_weights - delta_part[:, :, None])).astype(jnp.bfloat16)
    return (weights_now.astype(jnp.bfloat16), dscore)


def on_device(
    tokens,
    scene_tokens,
    cotangent,
    qkv_master,
    out_master,
    up_master,
    down_master,
    gain_one,
    gain_two,
):
    local_rows = tokens.shape[0]
    model_width = tokens.shape[1]
    live_count = scene_tokens[0]
    local_live = jnp.arange(local_rows, dtype=jnp.int32) < live_count
    qkv_part = qkv_master.astype(jnp.bfloat16)
    out_part = out_master.astype(jnp.bfloat16)
    up_part = up_master.astype(jnp.bfloat16)
    down_part = down_master.astype(jnp.bfloat16)
    qkv_weight, out_weight, up_weight, down_weight = (
        lax.all_gather(qkv_part, ("scene", "seq"), axis=0, tiled=True),
        lax.all_gather(out_part, ("scene", "seq"), axis=0, tiled=True),
        lax.all_gather(up_part, ("scene", "seq"), axis=0, tiled=True),
        lax.all_gather(down_part, ("scene", "seq"), axis=0, tiled=True),
    )
    inputs = tokens.astype(jnp.float32)
    normed_one, scaled_one, inverse_one = norm_rows(inputs, gain_one)
    normed_low = normed_one.astype(jnp.bfloat16)
    qkv_rows = jnp.dot(normed_low, qkv_weight, preferred_element_type=jnp.float32).astype(
        jnp.bfloat16
    )
    queries = qkv_rows[:, :model_width]
    key_rows = qkv_rows[:, model_width : 2 * model_width]
    value_rows = qkv_rows[:, 2 * model_width :]
    query_heads = split_heads(queries)

    def piece_live(piece_rows):
        places = jnp.arange(piece_rows, dtype=jnp.int32)
        return places % local_rows < live_count

    row_max = jnp.full((HEADS, local_rows), NEG_BIG, jnp.float32)
    key_piece = lax.all_gather(key_rows, "seq", axis=0, tiled=True)
    value_piece = lax.all_gather(value_rows, "seq", axis=0, tiled=True)
    piece_rows = key_piece.shape[0]
    scores = (
        jnp.einsum(
            "qhd,khd->hqk", query_heads, split_heads(key_piece), preferred_element_type=jnp.float32
        )
        * 0.125
    )
    scores = jnp.where(piece_live(piece_rows)[None, None, :], scores, NEG_BIG)
    new_max = jnp.maximum(row_max, jnp.max(scores, axis=-1))
    exponent = jnp.exp(scores - new_max[:, :, None])
    new_sum = jnp.sum(exponent, axis=-1)
    update = jnp.einsum(
        "hqk,khd->hqd",
        exponent.astype(jnp.bfloat16),
        split_heads(value_piece),
        preferred_element_type=jnp.float32,
    )
    row_lse = new_max + jnp.log(new_sum)
    attended = (
        (update / new_sum[:, :, None])
        .transpose(1, 0, 2)
        .reshape(local_rows, model_width)
        .astype(jnp.bfloat16)
    )
    resid = inputs + jnp.dot(attended, out_weight, preferred_element_type=jnp.float32)
    normed_two, scaled_two, inverse_two = norm_rows(resid, gain_two)
    normed_two_low = normed_two.astype(jnp.bfloat16)
    upper = jnp.dot(normed_two_low, up_weight, preferred_element_type=jnp.float32)
    activated, gelu_back = jax.vjp(jax.nn.gelu, upper)
    activated_low = activated.astype(jnp.bfloat16)
    mixed = (
        resid + jnp.dot(activated_low, down_weight, preferred_element_type=jnp.float32)
    ).astype(jnp.bfloat16)
    grad_result = cotangent.astype(jnp.float32) * local_live[:, None].astype(jnp.float32)
    grad_low = grad_result.astype(jnp.bfloat16)
    down_grad = jnp.einsum("tf,td->fd", activated_low, grad_low, preferred_element_type=jnp.float32)
    grad_active = jnp.einsum("td,fd->tf", grad_low, down_weight, preferred_element_type=jnp.float32)
    grad_upper = gelu_back(grad_active)[0].astype(jnp.bfloat16)
    up_grad = jnp.einsum(
        "td,tf->df", normed_two_low, grad_upper, preferred_element_type=jnp.float32
    )
    grad_normed_two = jnp.einsum(
        "tf,df->td", grad_upper, up_weight, preferred_element_type=jnp.float32
    )
    grad_norm_second, gain_two_grad = norm_back(grad_normed_two, scaled_two, inverse_two, gain_two)
    grad_resid = grad_result + grad_norm_second
    grad_branch = grad_resid.astype(jnp.bfloat16)
    out_grad = jnp.einsum("te,td->ed", attended, grad_branch, preferred_element_type=jnp.float32)
    grad_attended = jnp.einsum(
        "td,ed->te", grad_branch, out_weight, preferred_element_type=jnp.float32
    ).astype(jnp.bfloat16)
    grad_heads = split_heads(grad_attended)
    delta = jnp.sum(
        grad_heads.astype(jnp.float32) * split_heads(attended).astype(jnp.float32), axis=-1
    ).T
    total_rows = local_rows * lax.axis_size("seq")
    key_piece = lax.all_gather(key_rows, "seq", axis=0, tiled=True)
    value_piece = lax.all_gather(value_rows, "seq", axis=0, tiled=True)
    piece_rows = key_piece.shape[0]
    key_heads = split_heads(key_piece)
    weights_low, dscore = score_grads(
        query_heads,
        grad_heads,
        key_heads,
        split_heads(value_piece),
        row_lse,
        delta,
        piece_live(piece_rows),
    )
    grad_query = (
        jnp.einsum("hqk,khd->qhd", dscore, key_heads, preferred_element_type=jnp.float32) * 0.125
    )
    key_terms = (
        jnp.einsum("hqk,qhd->khd", dscore, query_heads, preferred_element_type=jnp.float32) * 0.125
    )
    value_terms = jnp.einsum(
        "hqk,qhd->khd", weights_low, grad_heads, preferred_element_type=jnp.float32
    )
    key_buffer = key_terms
    value_buffer = value_terms
    grad_query, key_buffer, value_buffer = (grad_query, key_buffer, value_buffer)
    grad_keys, grad_values = (
        lax.psum_scatter(
            key_buffer.reshape(total_rows, model_width).astype(jnp.bfloat16),
            "seq",
            scatter_dimension=0,
            tiled=True,
        ).astype(jnp.float32),
        lax.psum_scatter(
            value_buffer.reshape(total_rows, model_width).astype(jnp.bfloat16),
            "seq",
            scatter_dimension=0,
            tiled=True,
        ).astype(jnp.float32),
    )
    grad_qkv = jnp.concatenate(
        [grad_query.reshape(local_rows, model_width), grad_keys, grad_values], axis=1
    ).astype(jnp.bfloat16)
    qkv_grad = jnp.einsum("td,te->de", normed_low, grad_qkv, preferred_element_type=jnp.float32)
    grad_normed_one = jnp.einsum(
        "te,de->td", grad_qkv, qkv_weight, preferred_element_type=jnp.float32
    )
    grad_norm_first, gain_one_grad = norm_back(grad_normed_one, scaled_one, inverse_one, gain_one)
    input_grad = grad_resid + grad_norm_first
    qkv_share, out_share, up_share, down_share, first_share, second_share = (
        lax.psum_scatter(qkv_grad, ("scene", "seq"), scatter_dimension=0, tiled=True),
        lax.psum_scatter(out_grad, ("scene", "seq"), scatter_dimension=0, tiled=True),
        lax.psum_scatter(up_grad, ("scene", "seq"), scatter_dimension=0, tiled=True),
        lax.psum_scatter(down_grad, ("scene", "seq"), scatter_dimension=0, tiled=True),
        lax.psum_scatter(gain_one_grad, ("scene", "seq"), scatter_dimension=0, tiled=True),
        lax.psum_scatter(gain_two_grad, ("scene", "seq"), scatter_dimension=0, tiled=True),
    )
    return (
        mixed,
        input_grad,
        qkv_share,
        out_share,
        up_share,
        down_share,
        first_share,
        second_share,
    )


def solution(mesh):
    in_specs = (
        P(("scene", "seq"), None),
        P("scene"),
        P(("scene", "seq"), None),
        P(("scene", "seq"), None),
        P(("scene", "seq"), None),
        P(("scene", "seq"), None),
        P(("scene", "seq"), None),
        P(),
        P(),
    )
    out_specs = (
        P(("scene", "seq"), None),
        P(("scene", "seq"), None),
        P(("scene", "seq"), None),
        P(("scene", "seq"), None),
        P(("scene", "seq"), None),
        P(("scene", "seq"), None),
        P(("scene", "seq")),
        P(("scene", "seq")),
    )
    return jax.shard_map(
        on_device, mesh=mesh, in_specs=in_specs, out_specs=out_specs, check_vma=False
    )
```

profile of v0, /device:TPU:0, one launch (start us, length us, event | category | flops | bytes accessed | tf_op | source)
XLA Modules:
  0.0 1135.8 jit_solution(7848209360860348284)
XLA Ops:
  11.4 63.0 %all-gather.7.cloned.1.call-done = bf16[768,2304]{1,0:T(8,128)(2,1)} async-done(((bf16[24,2304]{1,0:T(8,128)(2,1)}), bf16[768,2304]{1,0:T(8,128)(2,1)}) %all-gather.7.cloned.1.call-update) | async-done | bytes 3538960 | tf_op jit(solution)/shard_map/all_gather | solution.py:64
  74.4 3.6 convolution_convert_fusion
  83.1 65.0 %all-gather.9.cloned.1.call-done = bf16[2560,768]{1,0:T(8,128)(2,1)} async-done(((bf16[320,768]{1,0:T(8,128)(2,1)}), bf16[2560,768]{1,0:T(8,128)(2,1)}) %all-gather.9.cloned.1.call-update) | async-done | bytes 3932176 | tf_op jit(solution)/shard_map/all_gather | solution.py:85
  148.1 6.3 copy.29
  154.4 17.1 %select_reduce_fusion = (f32[12,320]{1,0:T(8,128)S(1)}, f32[12,320,2560]{2,1,0:T(8,128)}) fusion(pred[2560]{0:T(1024)(128)(4,1)S(1)} %fusion.51, bf16[320,12,64]{0,2,1:T(8,128)(2,1)S(1)} %bitcast.50, bf16[2560,12,64]{0,2,1:T(8,128)(2,1)} %bitcast.47), kind=kOutput, calls=%fused_computation.3 | convolution fusion | flops 1287778560 | bytes 43763200 | tf_op jit(solution)/shard_map/qhd,khd->hqk/dot_general | solution.py:89
  171.5 47.9 %all-gather.11.cloned.1.call-done = bf16[2560,768]{1,0:T(8,128)(2,1)} async-done(((bf16[320,768]{1,0:T(8,128)(2,1)}), bf16[2560,768]{1,0:T(8,128)(2,1)}) %all-gather.11.cloned.1.call-update) | async-done | bytes 3932176 | tf_op jit(solution)/shard_map/all_gather | solution.py:86
  219.4 6.2 copy.30
  225.6 18.1 %fusion = f32[12,320]{1,0:T(8,128)S(1)} fusion(f32[12,320,2560]{2,1,0:T(8,128)} %get-tuple-element.20, f32[12,320]{1,0:T(8,128)S(1)} %broadcast_maximum_fusion, pred[2560]{0:T(1024)(128)(4,1)S(1)} %fusion.51), kind=kLoop, calls=%fused_computation.4 | loop fusion | flops 39317760 | bytes 39354880 | tf_op jit(solution)/shard_map/reduce_sum | solution.py:97
  243.8 15.2 %divide_convert_fusion = bf16[320,12,64]{0,2,1:T(8,128)(2,1)S(1)} fusion(bf16[2560,12,64]{0,2,1:T(8,128)(2,1)S(1)} %bitcast.55, f32[12,320,2560]{2,1,0:T(8,128)} %get-tuple-element.20, f32[12,320]{1,0:T(8,128)S(1)} %broadcast_maximum_fusion, pred[2560]{0:T(1024)(128)(4,1)S(1)} %fusion.51, f32[320,12]{0,1:T(8,128)S(1)} %bitcast.62), kind=kOutput, calls=%fused_computation.35 | convolution fusion | flops 1298104320 | bytes 43778560 | tf_op jit(solution)/shard_map/hqk,khd->hqd/dot_general | solution.py:98
  259.0 16.4 %all-gather.13.cloned.1.call-done = bf16[768,768]{1,0:T(8,128)(2,1)} async-done(((bf16[24,768]{1,0:T(8,128)(2,1)}), bf16[768,768]{1,0:T(8,128)(2,1)}) %all-gather.13.cloned.1.call-update) | async-done | bytes 1179664 | tf_op jit(solution)/shard_map/all_gather | solution.py:65
  278.2 63.0 %all-gather.15.cloned.1.call-done = bf16[768,3072]{1,0:T(8,128)(2,1)} async-done(((bf16[24,3072]{1,0:T(8,128)(2,1)}), bf16[768,3072]{1,0:T(8,128)(2,1)}) %all-gather.15.cloned.1.call-update) | async-done | bytes 4718608 | tf_op jit(solution)/shard_map/all_gather | solution.py:66
  341.3 6.0 fusion.65
  347.3 59.8 %all-gather.17.cloned.1.call-done = bf16[3072,768]{1,0:T(8,128)(2,1)} async-done(((bf16[96,768]{1,0:T(8,128)(2,1)}), bf16[3072,768]{1,0:T(8,128)(2,1)}) %all-gather.17.cloned.1.call-update) | async-done | bytes 4718608 | tf_op jit(solution)/shard_map/all_gather | solution.py:67
  407.1 7.8 fusion.18
  415.0 2.5 multiply_reduce_fusion.1
  419.5 18.2 %fusion.9 = bf16[12,64,2560]{2,1,0:T(8,128)(2,1)} fusion(bf16[320,12,64]{0,2,1:T(8,128)(2,1)} %bitcast.59, f32[12,320,2560]{2,1,0:T(8,128)} %get-tuple-element.20, f32[12,320]{1,0:T(8,128)} %log_add_fusion, pred[2560]{0:T(1024)(128)(4,1)S(1)} %fusion.51), kind=kOutput, calls=%fused_computation.14 | convolution fusion | flops 1299578880 | bytes 43763200 | tf_op jit(solution)/shard_map/hqk,qhd->khd/dot_general | solution.py:162
  437.7 6.3 copy.34
  445.6 26.5 %multiply_convert_fusion = bf16[12,320,2560]{2,1,0:T(8,128)(2,1)} fusion(f32[12,320,2560]{2,1,0:T(8,128)} %get-tuple-element.20, bf16[320,12,64]{0,2,1:T(8,128)(2,1)} %bitcast.61, bf16[2560,12,64]{0,2,1:T(8,128)(2,1)} %bitcast.54, f32[12,320]{1,0:T(8,128)S(1)} %bitcast.63, f32[12,320]{1,0:T(8,128)S(1)} %copy-done.19, pred[2560]{0:T(1024)(128)(4,1)S(1)} %fusion.51), kind=kOutput, calls=%fused_computation | convolution fusion | flops 1317273600 | bytes 63439360 | tf_op jit(solution)/shard_map/qhd,khd->hqk/dot_general | solution.py:37
  472.1 12.6 %multiply_convert_fusion.1 = bf16[12,64,2560]{2,1,0:T(8,128)(2,1)} fusion(bf16[320,12,64]{0,2,1:T(8,128)(2,1)S(1)} %bitcast.51, bf16[12,320,2560]{2,1,0:T(8,128)(2,1)} %multiply_convert_fusion), kind=kOutput, calls=%fused_computation.11 | convolution fusion | flops 1262223360 | bytes 24084480 | tf_op jit(solution)/shard_map/hqk,qhd->khd/dot_general | solution.py:160
  484.7 6.3 copy.32
  494.3 6.8 fusion.64
  502.2 8.7 fusion.45
  511.0 10.9 fusion.23
  522.0 5.4 reduce-scatter.21.cloned.1.call-done
  529.5 86.1 %reduce-scatter.19.cloned.1.call-done = bf16[320,768]{1,0:T(8,128)(2,1)} async-done(((bf16[2560,768]{1,0:T(8,128)(2,1)}), bf16[320,768]{1,0:T(8,128)(2,1)}) %reduce-scatter.19.cloned.1.call-update) | async-done | bytes 491536
  617.7 6.4 fusion.38
  624.1 6.9 fusion.22
  632.9 40.4 %all-reduce.2 = (f32[768]{0:T(1024)S(1)}, f32[768]{0:T(1024)S(1)}) all-reduce(f32[768]{0:T(1024)S(1)} %get-tuple-element.10, f32[768]{0:T(1024)S(1)} %copy-done.23), channel_id=8, replica_groups=mesh['scene'=4,'seq'=8] {'scene','seq'}, use_global_device_ids=true, to_apply=%region_18.19.clone | all-reduce | flops 1536 | bytes 12288
  675.8 44.5 %reduce-scatter.13.cloned.1.call-done = f32[24,768]{1,0:T(8,128)} async-done(((f32[768,768]{1,0:T(8,128)}), f32[24,768]{1,0:T(8,128)}) %reduce-scatter.13.cloned.1.call-update) | async-done | bytes 73744 | tf_op jit(solution)/shard_map/reduce_scatter | solution.py:193
  720.3 142.0 %reduce-scatter.15.cloned.1.call-done = f32[24,3072]{1,0:T(8,128)} async-done(((f32[768,3072]{1,0:T(8,128)}), f32[24,3072]{1,0:T(8,128)}) %reduce-scatter.15.cloned.1.call-update) | async-done | bytes 294928 | tf_op jit(solution)/shard_map/reduce_scatter | solution.py:194
  862.3 141.0 %reduce-scatter.17.cloned.1.call-done = f32[96,768]{1,0:T(8,128)} async-done(((f32[3072,768]{1,0:T(8,128)}), f32[96,768]{1,0:T(8,128)}) %reduce-scatter.17.cloned.1.call-update) | async-done | bytes 294928 | tf_op jit(solution)/shard_map/reduce_scatter | solution.py:195
  1003.3 125.4 %reduce-scatter.11.cloned.1.call-done = f32[24,2304]{1,0:T(8,128)} async-done(((f32[768,2304]{1,0:T(8,128)}), f32[24,2304]{1,0:T(8,128)}) %reduce-scatter.11.cloned.1.call-update) | async-done | bytes 221200 | tf_op jit(solution)/shard_map/reduce_scatter | solution.py:192
  (108 shorter events, 27.9 us)
Async XLA Ops:
  7.2 67.2 %all-gather.7.cloned.1.call-start = ((), (), s32[]{:S(2)}) async-start(), calls=%async_computation.6 | async-start | bytes 3649536 | tf_op jit(solution)/shard_map/all_gather | solution.py:64
  8.8 139.3 %all-gather.9.cloned.1.call-start = ((), (), s32[]{:S(2)}) async-start(), calls=%async_computation.7 | async-start | bytes 4423680 | tf_op jit(solution)/shard_map/all_gather | solution.py:85
  10.1 64.3 %copy-start.15 = (f32[320]{0:T(512)}, f32[320]{0:T(512)S(1)}, u32[]{:S(2)}) copy-start(f32[320]{0:T(512)S(1)} %broadcast_multiply_fusion.5) | copy-start | bytes 3844
  11.4 63.0 %copy-start.17 = (f32[320]{0:T(512)}, f32[320]{0:T(512)S(1)}, u32[]{:S(2)}) copy-start(f32[320]{0:T(512)S(1)} %add_rsqrt_fusion.1) | copy-start | bytes 3844
  78.0 2.6 copy-start.10
  78.0 3.3 copy-start.11
  79.1 140.3 %all-gather.11.cloned.1.call-start = ((), (), s32[]{:S(2)}) async-start(), calls=%async_computation.8 | async-start | bytes 4423680 | tf_op jit(solution)/shard_map/all_gather | solution.py:86
  79.8 195.6 %all-gather.13.cloned.1.call-start = ((), (), s32[]{:S(2)}) async-start(), calls=%async_computation.9 | async-start | bytes 1216512 | tf_op jit(solution)/shard_map/all_gather | solution.py:65
  80.5 260.8 %all-gather.15.cloned.1.call-start = ((), (), s32[]{:S(2)}) async-start(), calls=%async_computation.10 | async-start | bytes 4866048 | tf_op jit(solution)/shard_map/all_gather | solution.py:66
  81.3 325.8 %all-gather.17.cloned.1.call-start = ((), (), s32[]{:S(2)}) async-start(), calls=%async_computation.11 | async-start | bytes 4866048 | tf_op jit(solution)/shard_map/all_gather | solution.py:67
  82.0 445.4 %reduce-scatter.21.cloned.1.call-start = ((), (), s32[]{:S(2)}) async-start(), calls=%async_computation.17 | async-start | bytes 4423680
  82.8 324.4 %copy-start.20 = (f32[320]{0:T(512)}, f32[320]{0:T(512)S(1)}, u32[]{:S(2)}) copy-start(f32[320]{0:T(512)S(1)} %fusion.55) | copy-start | bytes 3844
  225.6 18.1 %copy-start.4 = (bf16[2560,768]{0,1:T(8,128)(2,1)S(1)}, bf16[2560,768]{0,1:T(8,128)(2,1)}, u32[]{:S(2)}) copy-start(bf16[2560,768]{0,1:T(8,128)(2,1)} %copy.30) | copy-start | bytes 11796484
  243.7 31.6 %copy-start = (bf16[320,768]{1,0:T(8,128)(2,1)S(1)}, bf16[320,768]{1,0:T(8,128)(2,1)}, u32[]{:S(2)}) copy-start(bf16[320,768]{1,0:T(8,128)(2,1)} %param.9) | copy-start | bytes 1474564
  259.0 88.3 %copy-start.1 = (bf16[320,12,64]{0,2,1:T(8,128)(2,1)}, bf16[320,12,64]{0,2,1:T(8,128)(2,1)S(1)}, u32[]{:S(2)}) copy-start(bf16[320,12,64]{0,2,1:T(8,128)(2,1)S(1)} %divide_convert_fusion) | copy-start | bytes 1474564
  259.0 82.3 %copy-start.12 = (f32[768]{0:T(1024)S(1)}, f32[768]{0:T(1024)}, u32[]{:S(2)}) copy-start(f32[768]{0:T(1024)} %param.17) | copy-start | bytes 9220
  278.2 128.9 %copy-start.8 = (bf16[320,768]{1,0:T(8,128)(2,1)S(1)}, bf16[320,768]{1,0:T(8,128)(2,1)}, u32[]{:S(2)}) copy-start(bf16[320,768]{1,0:T(8,128)(2,1)} %param.11) | copy-start | bytes 1474564
  407.1 7.8 copy-start.24
  415.0 2.5 copy-start.7
  415.0 2.5 copy-start.21
  415.0 2.9 copy-start.3
  444.1 171.5 %reduce-scatter.19.cloned.1.call-start = ((), (), s32[]{:S(2)}) async-start(), calls=%async_computation.16 | async-start | bytes 4423680
  491.0 229.3 %reduce-scatter.13.cloned.1.call-start = ((), (), s32[]{:S(2)}) async-start(), calls=%async_computation.13 | async-start | bytes 2433024 | tf_op jit(solution)/shard_map/reduce_scatter | solution.py:193
  494.3 368.1 %reduce-scatter.15.cloned.1.call-start = ((), (), s32[]{:S(2)}) async-start(), calls=%async_computation.14 | async-start | bytes 9732096 | tf_op jit(solution)/shard_map/reduce_scatter | solution.py:194
  501.2 502.1 %reduce-scatter.17.cloned.1.call-start = ((), (), s32[]{:S(2)}) async-start(), calls=%async_computation.15 | async-start | bytes 9732096 | tf_op jit(solution)/shard_map/reduce_scatter | solution.py:195
  511.0 106.7 %copy-start.13 = (f32[768]{0:T(1024)S(1)}, f32[768]{0:T(1024)}, u32[]{:S(2)}) copy-start(f32[768]{0:T(1024)} %param.16) | copy-start | bytes 9220
  511.0 106.7 %copy-start.16 = (f32[320]{0:T(512)S(1)}, f32[320]{0:T(512)}, u32[]{:S(2)}) copy-start(f32[320]{0:T(512)} %copy-done.15) | copy-start | bytes 3844
  511.0 106.7 %copy-start.18 = (f32[320]{0:T(512)S(1)}, f32[320]{0:T(512)}, u32[]{:S(2)}) copy-start(f32[320]{0:T(512)} %copy-done.17) | copy-start | bytes 3844
  511.0 617.7 %reduce-scatter.11.cloned.1.call-start = ((), (), s32[]{:S(2)}) async-start(), calls=%async_computation.12 | async-start | bytes 7299072 | tf_op jit(solution)/shard_map/reduce_scatter | solution.py:192
  624.1 6.9 copy-start.5
  624.1 6.9 copy-start.6
  624.1 6.9 copy-start.25
  (6 other events, 8.5 us)
Sparse Core Ops, SparseCore 0:
  11.5 62.8 all-gather.6
  79.2 68.8 all-gather.8
  150.9 68.4 all-gather.10
  222.7 52.6 all-gather.12
  278.7 62.5 all-gather.14
  344.6 62.4 all-gather.16
  444.2 83.1 reduce-scatter.20
  531.5 83.9 reduce-scatter.18
  621.4 98.8 reduce-scatter.12
  727.6 134.6 reduce-scatter.14
  868.8 134.4 reduce-scatter.16
  1010.4 118.2 reduce-scatter.10
where the time goes:
time: 1150 us; the launch traced here: 1140 us
  waiting for transfers between devices  860 us (75%)
  matrix products  156 us (14%)
  blocking collectives  40.4 us (4%)
  local copies, waits for them, and re-layouts  35 us (3%)
  other arithmetic  28.3 us (2%)
  between operations  15.4 us (1%)
    reduce_scatter x1, waiting for transfers between devices, on_device(): lax.psum_scatter(up_grad, ('scene', 'seq'), scatter_dimension=0, tiled=True)  142 us
    reduce_scatter x1, waiting for transfers between devices, on_device(): lax.psum_scatter(down_grad, ('scene', 'seq'), scatter_dimension=0, tiled=...  141 us
    reduce_scatter x1, waiting for transfers between devices, on_device(): lax.psum_scatter(qkv_grad, ('scene', 'seq'), scatter_dimension=0, tiled=T...  125 us
    unnamed x14, waiting for transfers between devices  92.4 us
    all_gather x1, waiting for transfers between devices, on_device(): key_piece = lax.all_gather(key_rows, 'seq', axis=0, tiled=True)  65 us
    all_gather x1, waiting for transfers between devices, on_device(): lax.all_gather(up_part, ('scene', 'seq'), axis=0, tiled=True)  63 us
    all_gather x1, waiting for transfers between devices, on_device(): lax.all_gather(qkv_part, ('scene', 'seq'), axis=0, tiled=True)  63 us
    all_gather x1, waiting for transfers between devices, on_device(): lax.all_gather(down_part, ('scene', 'seq'), axis=0, tiled=True)  59.8 us
  transfers between devices with their start and end apart: 12, of which 12 were waited for; matrix products, arithmetic and copies ran while one was open for 15% of the time, Pallas kernels for 0%

commit v1 on v0

--- a/solution.py
+++ b/solution.py
@@ -6,6 +6,17 @@
 HEADS = 12
 HEAD = 64
 NEG_BIG = -1e30
+
+
+def turned_line(x, name, along):
+    size = lax.axis_size(name)
+    right = [(i, (i + 1) % size) for i in range(size)]
+    parts = [x]
+    for stride in range(1, size):
+        parts = [lax.ppermute(parts[0], name, right), *parts]
+    whole = jnp.concatenate(parts, axis=along)
+    shift = (lax.axis_index(name) + 1) * parts[-1].shape[along]
+    return jnp.roll(whole, shift, axis=along)
 
 
 def norm_rows(values, gain_vector):
@@ -82,7 +93,7 @@
         return places % local_rows < live_count
 
     row_max = jnp.full((HEADS, local_rows), NEG_BIG, jnp.float32)
-    key_piece = lax.all_gather(key_rows, "seq", axis=0, tiled=True)
+    key_piece = turned_line(key_rows, "seq", 0)
     value_piece = lax.all_gather(value_rows, "seq", axis=0, tiled=True)
     piece_rows = key_piece.shape[0]
     scores = (

time: 1150 us -> 1230 us (1.070)
  waiting for transfers between devices: 860 us -> 915 us
  matrix products: 156 us -> 173 us
  local copies, waits for them, and re-layouts: 35 us -> 50.7 us
    ppermute x0 -> x7, waiting for transfers between devices: none -> 136 us  [turned_line(): parts = [lax.ppermute(parts[0], name, right), *parts]]
    all_gather x1, waiting for transfers between devices: 65 us -> 0.01 us  [on_device(): key_piece = lax.all_gather(key_rows, 'seq', axis=0, tiled=True)]
    all_gather x1, waiting for transfers between devices: 47.9 us -> 0.01 us  [on_device(): value_piece = lax.all_gather(value_rows, 'seq', axis=0, tiled=True)]
    unnamed x14, waiting for transfers between devices: 92.4 us -> 114 us
    dot_general x0 -> x1, matrix products: none -> 16.8 us  [score_grads(): jnp.einsum('qhd,khd->hqk', query_part, key_part, preferred_element_type=j...]
  transfers between devices with their start and end apart: 12 -> 19, of which waited for: 12 -> 17; matrix products, arithmetic and copies ran while one was open for 15% -> 15% of each run, Pallas kernels for 0% -> 0%
where the time goes in v1:
time: 1230 us
  waiting for transfers between devices  915 us (74%)
  matrix products  173 us (14%)
  local copies, waits for them, and re-layouts  50.7 us (4%)
  blocking collectives  40.4 us (3%)
  other arithmetic  28 us (2%)
  between operations  15.6 us (1%)
    reduce_scatter x1, waiting for transfers between devices, on_device(): lax.psum_scatter(down_grad, ('scene', 'seq'), scatter_dimension=0, tiled=...  142 us
    reduce_scatter x1, waiting for transfers between devices, on_device(): lax.psum_scatter(up_grad, ('scene', 'seq'), scatter_dimension=0, tiled=True)  141 us
    ppermute x7, waiting for transfers between devices, turned_line(): parts = [lax.ppermute(parts[0], name, right), *parts]  136 us
    reduce_scatter x1, waiting for transfers between devices, on_device(): lax.psum_scatter(qkv_grad, ('scene', 'seq'), scatter_dimension=0, tiled=T...  125 us
    unnamed x14, waiting for transfers between devices  114 us
    all_gather x1, waiting for transfers between devices, on_device(): lax.all_gather(up_part, ('scene', 'seq'), axis=0, tiled=True)  63.7 us
    all_gather x1, waiting for transfers between devices, on_device(): lax.all_gather(qkv_part, ('scene', 'seq'), axis=0, tiled=True)  63 us
    all_gather x1, waiting for transfers between devices, on_device(): lax.all_gather(down_part, ('scene', 'seq'), axis=0, tiled=True)  59.9 us
  transfers between devices with their start and end apart: 19, of which 17 were waited for; matrix products, arithmetic and copies ran while one was open for 15% of the time, Pallas kernels for 0%

profile of v1, /device:TPU:0, one launch (start us, length us, event | category | flops | bytes accessed | tf_op | source)
XLA Modules:
  0.0 1226.2 jit_solution(2161179494009830598)
XLA Ops:
  11.4 63.0 %all-gather.7.cloned.1.call-done = bf16[768,2304]{1,0:T(8,128)(2,1)} async-done(((bf16[24,2304]{1,0:T(8,128)(2,1)}), bf16[768,2304]{1,0:T(8,128)(2,1)}) %all-gather.7.cloned.1.call-update) | async-done | bytes 3538960 | tf_op jit(solution)/shard_map/all_gather | solution.py:75
  80.4 19.1 %collective-permute-done = bf16[320,768]{1,0:T(8,128)(2,1)S(1)} collective-permute-done((bf16[320,768]{1,0:T(8,128)(2,1)}, bf16[320,768]{1,0:T(8,128)(2,1)S(1)}, u32[]{:S(2)}, u32[]{:S(2)}) %collective-permute-start) | collective-permute-done | bytes 491552 | tf_op jit(solution)/shard_map/ppermute | solution.py:16
  99.5 22.1 %collective-permute-done.1 = bf16[320,768]{1,0:T(8,128)(2,1)S(1)} collective-permute-done((bf16[320,768]{1,0:T(8,128)(2,1)S(1)}, bf16[320,768]{1,0:T(8,128)(2,1)S(1)}, u32[]{:S(2)}, u32[]{:S(2)}) %collective-permute-start.1) | collective-permute-done | bytes 491552 | tf_op jit(solution)/shard_map/ppermute | solution.py:16
  121.6 26.6 %collective-permute-done.2 = bf16[320,768]{1,0:T(8,128)(2,1)S(1)} collective-permute-done((bf16[320,768]{1,0:T(8,128)(2,1)S(1)}, bf16[320,768]{1,0:T(8,128)(2,1)S(1)}, u32[]{:S(2)}, u32[]{:S(2)}) %collective-permute-start.2) | collective-permute-done | bytes 491552 | tf_op jit(solution)/shard_map/ppermute | solution.py:16
  148.2 26.4 %collective-permute-done.3 = bf16[320,768]{1,0:T(8,128)(2,1)S(1)} collective-permute-done((bf16[320,768]{1,0:T(8,128)(2,1)S(1)}, bf16[320,768]{1,0:T(8,128)(2,1)S(1)}, u32[]{:S(2)}, u32[]{:S(2)}) %collective-permute-start.3) | collective-permute-done | bytes 491552 | tf_op jit(solution)/shard_map/ppermute | solution.py:16
  174.6 14.8 %collective-permute-done.4 = bf16[320,768]{1,0:T(8,128)(2,1)S(1)} collective-permute-done((bf16[320,768]{1,0:T(8,128)(2,1)S(1)}, bf16[320,768]{1,0:T(8,128)(2,1)S(1)}, u32[]{:S(2)}, u32[]{:S(2)}) %collective-permute-start.4) | collective-permute-done | bytes 491552 | tf_op jit(solution)/shard_map/ppermute | solution.py:16
  189.5 13.9 %collective-permute-done.5 = bf16[320,768]{1,0:T(8,128)(2,1)S(1)} collective-permute-done((bf16[320,768]{1,0:T(8,128)(2,1)S(1)}, bf16[320,768]{1,0:T(8,128)(2,1)S(1)}, u32[]{:S(2)}, u32[]{:S(2)}) %collective-permute-start.5) | collective-permute-done | bytes 491552 | tf_op jit(solution)/shard_map/ppermute | solution.py:16
  203.4 13.0 %collective-permute-done.6 = bf16[320,768]{1,0:T(8,128)(2,1)S(1)} collective-permute-done((bf16[320,768]{1,0:T(8,128)(2,1)S(1)}, bf16[320,768]{1,0:T(8,128)(2,1)S(1)}, u32[]{:S(2)}, u32[]{:S(2)}) %collective-permute-start.6) | collective-permute-done | bytes 491552 | tf_op jit(solution)/shard_map/ppermute | solution.py:16
  236.3 17.5 %fusion = (f32[12,320]{1,0:T(8,128)S(1)}, f32[12,320,2560]{2,1,0:T(8,128)}) fusion(pred[2560]{0:T(1024)(128)(4,1)S(1)} %fusion.52, bf16[320,12,64]{0,2,1:T(8,128)(2,1)S(1)} %bitcast.54, bf16[2560,12,64]{0,2,1:T(8,128)(2,1)} %bitcast.52), kind=kOutput, calls=%fused_computation.4 | convolution fusion | flops 1287778560 | bytes 43763200 | tf_op jit(solution)/shard_map/qhd,khd->hqk/dot_general | solution.py:100
  253.9 17.8 %fusion.1 = f32[12,320]{1,0:T(8,128)S(1)} fusion(f32[12,320,2560]{2,1,0:T(8,128)} %get-tuple-element.20, f32[12,320]{1,0:T(8,128)S(1)} %broadcast_maximum_fusion, pred[2560]{0:T(1024)(128)(4,1)S(1)} %fusion.52), kind=kLoop, calls=%fused_computation.5 | loop fusion | flops 39317760 | bytes 39354880 | tf_op jit(solution)/shard_map/reduce_sum | solution.py:108
  278.5 16.8 %fusion.68 = f32[12,320,2560]{2,1,0:T(8,128)} fusion(bf16[320,12,64]{0,2,1:T(8,128)(2,1)S(1)} %bitcast.55, bf16[2560,12,64]{0,2,1:T(8,128)(2,1)} %bitcast.50), kind=kOutput, calls=%fused_computation.111 | convolution fusion | flops 1258291200 | bytes 43745280 | tf_op jit(solution)/shard_map/qhd,khd->hqk/dot_general | solution.py:45
  301.6 16.4 %divide_convert_fusion = bf16[320,12,64]{0,2,1:T(8,128)(2,1)S(1)} fusion(bf16[2560,12,64]{0,2,1:T(8,128)(2,1)} %bitcast.59, f32[12,320,2560]{2,1,0:T(8,128)} %get-tuple-element.20, f32[12,320]{1,0:T(8,128)S(1)} %broadcast_maximum_fusion, pred[2560]{0:T(1024)(128)(4,1)S(1)} %fusion.52, f32[320,12]{0,1:T(8,128)S(1)} %bitcast.67), kind=kOutput, calls=%fused_computation.36 | convolution fusion | flops 1298104320 | bytes 43778560 | tf_op jit(solution)/shard_map/hqk,khd->hqd/dot_general | solution.py:109
  318.0 26.5 %all-gather.11.cloned.1.call-done = bf16[768,768]{1,0:T(8,128)(2,1)} async-done(((bf16[24,768]{1,0:T(8,128)(2,1)}), bf16[768,768]{1,0:T(8,128)(2,1)}) %all-gather.11.cloned.1.call-update) | async-done | bytes 1179664 | tf_op jit(solution)/shard_map/all_gather | solution.py:76
  346.8 63.7 %all-gather.13.cloned.1.call-done = bf16[768,3072]{1,0:T(8,128)(2,1)} async-done(((bf16[24,3072]{1,0:T(8,128)(2,1)}), bf16[768,3072]{1,0:T(8,128)(2,1)}) %all-gather.13.cloned.1.call-update) | async-done | bytes 4718608 | tf_op jit(solution)/shard_map/all_gather | solution.py:77
  416.4 59.9 %all-gather.15.cloned.1.call-done = bf16[3072,768]{1,0:T(8,128)(2,1)} async-done(((bf16[96,768]{1,0:T(8,128)(2,1)}), bf16[3072,768]{1,0:T(8,128)(2,1)}) %all-gather.15.cloned.1.call-update) | async-done | bytes 4718608 | tf_op jit(solution)/shard_map/all_gather | solution.py:78
  476.3 7.4 fusion.19
  489.7 26.1 %multiply_convert_fusion = bf16[12,320,2560]{2,1,0:T(8,128)(2,1)} fusion(f32[12,320,2560]{2,1,0:T(8,128)} %fusion.68, bf16[320,12,64]{0,2,1:T(8,128)(2,1)} %bitcast.65, bf16[2560,12,64]{0,2,1:T(8,128)(2,1)} %bitcast.60, f32[12,320]{1,0:T(8,128)S(1)} %bitcast.68, f32[12,320]{1,0:T(8,128)} %log_add_fusion, pred[2560]{0:T(1024)(128)(4,1)S(1)} %fusion.52), kind=kOutput, calls=%fused_computation | convolution fusion | flops 1317273600 | bytes 63439360 | tf_op jit(solution)/shard_map/qhd,khd->hqk/dot_general | solution.py:48
  515.8 12.4 %multiply_convert_fusion.1 = bf16[12,64,2560]{2,1,0:T(8,128)(2,1)} fusion(bf16[320,12,64]{0,2,1:T(8,128)(2,1)S(1)} %bitcast.56, bf16[12,320,2560]{2,1,0:T(8,128)(2,1)} %multiply_convert_fusion), kind=kOutput, calls=%fused_computation.12 | convolution fusion | flops 1262223360 | bytes 24084480 | tf_op jit(solution)/shard_map/hqk,qhd->khd/dot_general | solution.py:171
  535.6 18.3 %fusion.10 = bf16[12,64,2560]{2,1,0:T(8,128)(2,1)} fusion(bf16[320,12,64]{0,2,1:T(8,128)(2,1)S(1)} %bitcast.66, f32[12,320,2560]{2,1,0:T(8,128)} %fusion.68, f32[12,320]{1,0:T(8,128)S(1)} %copy-done.20, pred[2560]{0:T(1024)(128)(4,1)S(1)} %fusion.52), kind=kOutput, calls=%fused_computation.15 | convolution fusion | flops 1299578880 | bytes 43763200 | tf_op jit(solution)/shard_map/hqk,qhd->khd/dot_general | solution.py:173
  553.8 6.3 copy.37
  563.5 8.8 fusion.46
  572.4 6.8 fusion.65
  579.3 11.1 fusion.24
  590.4 27.4 %reduce-scatter.19.cloned.1.call-done = bf16[320,768]{1,0:T(8,128)(2,1)} async-done(((bf16[2560,768]{1,0:T(8,128)(2,1)}), bf16[320,768]{1,0:T(8,128)(2,1)}) %reduce-scatter.19.cloned.1.call-update) | async-done | bytes 491536
  619.9 86.1 %reduce-scatter.21.cloned.1.call-done = bf16[320,768]{1,0:T(8,128)(2,1)} async-done(((bf16[2560,768]{1,0:T(8,128)(2,1)}), bf16[320,768]{1,0:T(8,128)(2,1)}) %reduce-scatter.21.cloned.1.call-update) | async-done | bytes 491536
  708.1 6.4 fusion.39
  714.5 6.9 fusion.23
  723.4 40.4 %all-reduce.2 = (f32[768]{0:T(1024)S(1)}, f32[768]{0:T(1024)S(1)}) all-reduce(f32[768]{0:T(1024)S(1)} %get-tuple-element.10, f32[768]{0:T(1024)S(1)} %copy-done.24), channel_id=8, replica_groups=mesh['scene'=4,'seq'=8] {'scene','seq'}, use_global_device_ids=true, to_apply=%region_18.19.clone | all-reduce | flops 1536 | bytes 12288
  766.2 44.5 %reduce-scatter.13.cloned.1.call-done = f32[24,768]{1,0:T(8,128)} async-done(((f32[768,768]{1,0:T(8,128)}), f32[24,768]{1,0:T(8,128)}) %reduce-scatter.13.cloned.1.call-update) | async-done | bytes 73744 | tf_op jit(solution)/shard_map/reduce_scatter | solution.py:204
  810.8 141.8 %reduce-scatter.17.cloned.1.call-done = f32[96,768]{1,0:T(8,128)} async-done(((f32[3072,768]{1,0:T(8,128)}), f32[96,768]{1,0:T(8,128)}) %reduce-scatter.17.cloned.1.call-update) | async-done | bytes 294928 | tf_op jit(solution)/shard_map/reduce_scatter | solution.py:206
  952.5 141.1 %reduce-scatter.15.cloned.1.call-done = f32[24,3072]{1,0:T(8,128)} async-done(((f32[768,3072]{1,0:T(8,128)}), f32[24,3072]{1,0:T(8,128)}) %reduce-scatter.15.cloned.1.call-update) | async-done | bytes 294928 | tf_op jit(solution)/shard_map/reduce_scatter | solution.py:205
  1093.7 125.4 %reduce-scatter.11.cloned.1.call-done = f32[24,2304]{1,0:T(8,128)} async-done(((f32[768,2304]{1,0:T(8,128)}), f32[24,2304]{1,0:T(8,128)}) %reduce-scatter.11.cloned.1.call-update) | async-done | bytes 221200 | tf_op jit(solution)/shard_map/reduce_scatter | solution.py:203
  (143 shorter events, 75.9 us)
Async XLA Ops:
  7.2 67.2 %all-gather.7.cloned.1.call-start = ((), (), s32[]{:S(2)}) async-start(), calls=%async_computation.6 | async-start | bytes 3649536 | tf_op jit(solution)/shard_map/all_gather | solution.py:75
  8.8 263.5 %all-gather.17.cloned.1.call-start = ((), (), s32[]{:S(2)}) async-start(), calls=%async_computation.11 | async-start | bytes 4423680 | tf_op jit(solution)/shard_map/all_gather | solution.py:154
  10.1 67.9 %copy-start.16 = (f32[320]{0:T(512)}, f32[320]{0:T(512)S(1)}, u32[]{:S(2)}) copy-start(f32[320]{0:T(512)S(1)} %broadcast_multiply_fusion.5) | copy-start | bytes 3844
  11.4 66.6 %copy-start.18 = (f32[320]{0:T(512)}, f32[320]{0:T(512)S(1)}, u32[]{:S(2)}) copy-start(f32[320]{0:T(512)S(1)} %add_rsqrt_fusion.1) | copy-start | bytes 3844
  78.8 216.5 %all-gather.9.cloned.1.call-start = ((), (), s32[]{:S(2)}) async-start(), calls=%async_computation.7 | async-start | bytes 4423680 | tf_op jit(solution)/shard_map/all_gather | solution.py:97
  78.9 20.6 %collective-permute-start = (bf16[320,768]{1,0:T(8,128)(2,1)}, bf16[320,768]{1,0:T(8,128)(2,1)S(1)}, u32[]{:S(2)}, u32[]{:S(2)}) collective-permute-start(bf16[320,768]{1,0:T(8,128)(2,1)} %slice.13), channel_id=1, source_target_pairs={{0,1},{1,2},{2,3},{3,4},{4,5},{5,6},{6,7},{7,0},{8,9},{9,10},{10,1... | collective-permute-start | bytes 1474568 | tf_op jit(solution)/shard_map/ppermute | solution.py:16
  99.5 22.1 %collective-permute-start.1 = (bf16[320,768]{1,0:T(8,128)(2,1)S(1)}, bf16[320,768]{1,0:T(8,128)(2,1)S(1)}, u32[]{:S(2)}, u32[]{:S(2)}) collective-permute-start(bf16[320,768]{1,0:T(8,128)(2,1)S(1)} %collective-permute-done), channel_id=1, source_target_pairs={{0,1},{1,2},{2,3},{3,4},{4,5},{5,6},{6,7},{7,0},{8,9},{9,10},{10,1... | collective-permute-start | bytes 1474568 | tf_op jit(solution)/shard_map/ppermute | solution.py:16
  121.6 26.6 %collective-permute-start.2 = (bf16[320,768]{1,0:T(8,128)(2,1)S(1)}, bf16[320,768]{1,0:T(8,128)(2,1)S(1)}, u32[]{:S(2)}, u32[]{:S(2)}) collective-permute-start(bf16[320,768]{1,0:T(8,128)(2,1)S(1)} %collective-permute-done.1), channel_id=1, source_target_pairs={{0,1},{1,2},{2,3},{3,4},{4,5},{5,6},{6,7},{7,0},{8,9},{9,10},{10,1... | collective-permute-start | bytes 1474568 | tf_op jit(solution)/shard_map/ppermute | solution.py:16
  148.2 26.4 %collective-permute-start.3 = (bf16[320,768]{1,0:T(8,128)(2,1)S(1)}, bf16[320,768]{1,0:T(8,128)(2,1)S(1)}, u32[]{:S(2)}, u32[]{:S(2)}) collective-permute-start(bf16[320,768]{1,0:T(8,128)(2,1)S(1)} %collective-permute-done.2), channel_id=1, source_target_pairs={{0,1},{1,2},{2,3},{3,4},{4,5},{5,6},{6,7},{7,0},{8,9},{9,10},{10,1... | collective-permute-start | bytes 1474568 | tf_op jit(solution)/shard_map/ppermute | solution.py:16
  174.6 14.8 %collective-permute-start.4 = (bf16[320,768]{1,0:T(8,128)(2,1)S(1)}, bf16[320,768]{1,0:T(8,128)(2,1)S(1)}, u32[]{:S(2)}, u32[]{:S(2)}) collective-permute-start(bf16[320,768]{1,0:T(8,128)(2,1)S(1)} %collective-permute-done.3), channel_id=1, source_target_pairs={{0,1},{1,2},{2,3},{3,4},{4,5},{5,6},{6,7},{7,0},{8,9},{9,10},{10,1... | collective-permute-start | bytes 1474568 | tf_op jit(solution)/shard_map/ppermute | solution.py:16
  189.5 13.9 %collective-permute-start.5 = (bf16[320,768]{1,0:T(8,128)(2,1)S(1)}, bf16[320,768]{1,0:T(8,128)(2,1)S(1)}, u32[]{:S(2)}, u32[]{:S(2)}) collective-permute-start(bf16[320,768]{1,0:T(8,128)(2,1)S(1)} %collective-permute-done.4), channel_id=1, source_target_pairs={{0,1},{1,2},{2,3},{3,4},{4,5},{5,6},{6,7},{7,0},{8,9},{9,10},{10,1... | collective-permute-start | bytes 1474568 | tf_op jit(solution)/shard_map/ppermute | solution.py:16
  203.4 13.0 %collective-permute-start.6 = (bf16[320,768]{1,0:T(8,128)(2,1)S(1)}, bf16[320,768]{1,0:T(8,128)(2,1)S(1)}, u32[]{:S(2)}, u32[]{:S(2)}) collective-permute-start(bf16[320,768]{1,0:T(8,128)(2,1)S(1)} %collective-permute-done.5), channel_id=1, source_target_pairs={{0,1},{1,2},{2,3},{3,4},{4,5},{5,6},{6,7},{7,0},{8,9},{9,10},{10,1... | collective-permute-start | bytes 1474568 | tf_op jit(solution)/shard_map/ppermute | solution.py:16
  221.0 123.6 %all-gather.11.cloned.1.call-start = ((), (), s32[]{:S(2)}) async-start(), calls=%async_computation.8 | async-start | bytes 1216512 | tf_op jit(solution)/shard_map/all_gather | solution.py:76
  221.7 188.8 %all-gather.13.cloned.1.call-start = ((), (), s32[]{:S(2)}) async-start(), calls=%async_computation.9 | async-start | bytes 4866048 | tf_op jit(solution)/shard_map/all_gather | solution.py:77
  222.5 253.9 %all-gather.15.cloned.1.call-start = ((), (), s32[]{:S(2)}) async-start(), calls=%async_computation.10 | async-start | bytes 4866048 | tf_op jit(solution)/shard_map/all_gather | solution.py:78
  223.2 394.6 %reduce-scatter.19.cloned.1.call-start = ((), (), s32[]{:S(2)}) async-start(), calls=%async_computation.16 | async-start | bytes 4423680
  224.5 251.8 %copy-start.21 = (f32[320]{0:T(512)}, f32[320]{0:T(512)S(1)}, u32[]{:S(2)}) copy-start(f32[320]{0:T(512)S(1)} %fusion.56) | copy-start | bytes 3844
  301.6 42.9 %copy-start = (bf16[320,768]{1,0:T(8,128)(2,1)S(1)}, bf16[320,768]{1,0:T(8,128)(2,1)}, u32[]{:S(2)}) copy-start(bf16[320,768]{1,0:T(8,128)(2,1)} %param.9) | copy-start | bytes 1474564
  318.0 98.4 %copy-start.1 = (bf16[320,12,64]{0,2,1:T(8,128)(2,1)}, bf16[320,12,64]{0,2,1:T(8,128)(2,1)S(1)}, u32[]{:S(2)}) copy-start(bf16[320,12,64]{0,2,1:T(8,128)(2,1)S(1)} %divide_convert_fusion) | copy-start | bytes 1474564
  318.0 92.4 %copy-start.13 = (f32[768]{0:T(1024)S(1)}, f32[768]{0:T(1024)}, u32[]{:S(2)}) copy-start(f32[768]{0:T(1024)} %param.17) | copy-start | bytes 9220
  346.8 129.5 %copy-start.9 = (bf16[320,768]{1,0:T(8,128)(2,1)S(1)}, bf16[320,768]{1,0:T(8,128)(2,1)}, u32[]{:S(2)}) copy-start(bf16[320,768]{1,0:T(8,128)(2,1)} %param.11) | copy-start | bytes 1474564
  476.3 7.4 copy-start.25
  534.5 171.5 %reduce-scatter.21.cloned.1.call-start = ((), (), s32[]{:S(2)}) async-start(), calls=%async_computation.17 | async-start | bytes 4423680
  560.2 250.5 %reduce-scatter.13.cloned.1.call-start = ((), (), s32[]{:S(2)}) async-start(), calls=%async_computation.13 | async-start | bytes 2433024 | tf_op jit(solution)/shard_map/reduce_scatter | solution.py:204
  563.5 389.1 %reduce-scatter.17.cloned.1.call-start = ((), (), s32[]{:S(2)}) async-start(), calls=%async_computation.15 | async-start | bytes 9732096 | tf_op jit(solution)/shard_map/reduce_scatter | solution.py:206
  572.3 521.3 %reduce-scatter.15.cloned.1.call-start = ((), (), s32[]{:S(2)}) async-start(), calls=%async_computation.14 | async-start | bytes 9732096 | tf_op jit(solution)/shard_map/reduce_scatter | solution.py:205
  579.2 128.8 %copy-start.14 = (f32[768]{0:T(1024)S(1)}, f32[768]{0:T(1024)}, u32[]{:S(2)}) copy-start(f32[768]{0:T(1024)} %param.16) | copy-start | bytes 9220
  579.2 128.8 %copy-start.17 = (f32[320]{0:T(512)S(1)}, f32[320]{0:T(512)}, u32[]{:S(2)}) copy-start(f32[320]{0:T(512)} %copy-done.16) | copy-start | bytes 3844
  579.3 128.8 %copy-start.19 = (f32[320]{0:T(512)S(1)}, f32[320]{0:T(512)}, u32[]{:S(2)}) copy-start(f32[320]{0:T(512)} %copy-done.18) | copy-start | bytes 3844
  579.3 639.8 %reduce-scatter.11.cloned.1.call-start = ((), (), s32[]{:S(2)}) async-start(), calls=%async_computation.12 | async-start | bytes 7299072 | tf_op jit(solution)/shard_map/reduce_scatter | solution.py:203
  714.5 6.9 copy-start.5
  714.5 6.9 copy-start.6
  (14 other events, 44.4 us)
Sparse Core Ops, SparseCore 0:
  11.5 62.8 all-gather.6
  78.9 95.1 all-gather.16
  221.1 67.4 all-gather.8
  292.0 52.5 all-gather.10
  347.9 62.5 all-gather.12
  413.8 62.4 all-gather.14
  534.6 83.1 reduce-scatter.18
  622.0 83.9 reduce-scatter.20
  711.9 98.8 reduce-scatter.12
  818.1 134.3 reduce-scatter.16
  959.0 134.6 reduce-scatter.14
  1100.7 118.2 reduce-scatter.10
